TPU v7x, 32 devices: a whole 2x2x4 slice. The times are simulated.
32 devices in a mesh: prow: 4 (over y, core), pcol: 8 (over z, x).
Axes of the slice: x: 2, y: 2, z: 4, core: 2. Of those that a mesh axis runs over, the one named last changes fastest.
Arguments:
- ainv: bfloat16 [8192, 8192], P('prow', 'pcol'), may hold values from -6 to 6
- panels: bfloat16 [3, 8192, 128], P(None, ('prow', 'pcol')), may hold values from -0.0625 to 0.0625
- structure: int32 [3, 64], replicated, may hold values from 0 to 1, as said below
- dinv: float32 [3, 128, 128], replicated, may hold values from -6 to 6
- couple: bfloat16 [2, 128, 128], replicated, may hold values from -0.5 to 0.5
Outputs:
- inv_panels: float32 [3, 8192, 128], P(None, ('prow', 'pcol'))
- inv_parent: float32 [2, 128, 128], replicated
- inv_diag: float32 [3, 128, 128], replicated
Inputs may be any that keep to these rules, and one draw needn't show every extreme that they name: Entries are 0 or 1; a block in the structure of step k+1 is also in that of step k.
All inputs are finite; a program needn't handle non-finite values.
Results may differ from a plain program's by a relative error of at most 0.0003.
Values may be sent and summed in bfloat16 or wider, within the bound.
No kernel may reach another device: no remote copies, remote signals or barrier semaphores. Data moves between devices by JAX's collectives and lax.ppermute only.
A program may use at most 64 MiB of HBM per device.

v0:
```python
import jax
import jax.numpy as jnp
from jax import lax
from jax.sharding import PartitionSpec as P


def broadcast(value, axis, source):
    kept = jnp.where(lax.axis_index(axis) == source, value, 0).astype(value.dtype)
    return lax.psum(kept, axis)


def shards(ainv, panels, structure, dinv, couple):
    high = lax.Precision.HIGHEST
    n_col = lax.axis_size("pcol")
    seg_rows = panels.shape[1]
    width_cols = panels.shape[2]
    sections = panels.shape[0]
    col_span = ainv.shape[1]
    height = ainv.shape[0]
    flat_index = lax.axis_index("prow") * n_col + lax.axis_index("pcol")
    row_ids = flat_index * seg_rows + jnp.arange(seg_rows, dtype=jnp.int32)
    block_ids = jnp.arange(structure.shape[1], dtype=jnp.int32)
    onehot = (row_ids[:, None] // width_cols == block_ids[None, :]).astype(jnp.float32)
    live_rows = jnp.einsum("rb,kb->kr", onehot, structure.astype(jnp.float32))
    factor = panels * live_rows[:, :, None].astype(jnp.bfloat16)
    column = lax.axis_index("pcol")
    offset = column * col_span % height
    owner = column * col_span // height
    products = []
    for section in range(sections):
        gathered = lax.all_gather(factor[section], "pcol", axis=0, tiled=True)
        wanted = lax.dynamic_slice_in_dim(gathered, offset, col_span, 0)
        received = broadcast(wanted, "prow", owner)

        def single_term(row_start, row_count, panel_cols=received):
            return jnp.dot(ainv, panel_cols, preferred_element_type=jnp.float32)

        products.append(
            lax.psum_scatter(
                single_term(jnp.int32(0), seg_rows * lax.axis_size("pcol")),
                "pcol",
                scatter_dimension=0,
                tiled=True,
            )
        )
    factor_wide = factor.astype(jnp.float32)
    couple_wide = couple.astype(jnp.float32)
    first_block = -products[0] * live_rows[0][:, None]
    first_local = jnp.dot(factor_wide[0].T, first_block, precision=high)
    diag_now = dinv[0] - lax.psum(first_local, ("prow", "pcol"))
    blocks_out = [first_block]
    diag_out = [diag_now]
    cross_out = []
    for section in range(1, sections):
        previous = blocks_out[-1]
        current = (
            -(products[section] + jnp.dot(previous, couple_wide[section - 1], precision=high))
            * live_rows[section][:, None]
        )
        own_term = jnp.dot(factor_wide[section].T, current, precision=high)
        cross_term = jnp.dot(previous.T, factor_wide[section], precision=high)
        own_sum, cross_sum = lax.psum((own_term, cross_term), ("prow", "pcol"))
        cross = -(cross_sum + jnp.dot(diag_now, couple_wide[section - 1], precision=high))
        diag_now = (
            dinv[section] - own_sum - jnp.dot(couple_wide[section - 1].T, cross, precision=high)
        )
        blocks_out.append(current)
        cross_out.append(cross)
        diag_out.append(diag_now)
    return (jnp.stack(blocks_out), jnp.stack(cross_out), jnp.stack(diag_out))


def solution(mesh):
    return jax.shard_map(
        shards,
        mesh=mesh,
        in_specs=(P("prow", "pcol"), P(None, ("prow", "pcol"), None), P(), P(), P()),
        out_specs=(P(None, ("prow", "pcol"), None), P(), P()),
        check_vma=False,
    )
```

profile of v0, /device:TPU:8, one launch (start us, length us, event | category | flops | bytes accessed | tf_op | source)
XLA Modules:
  0.0 495.4 jit_solution(17148334694424355662)
XLA Ops:
  7.2 0.0 all-reduce.7.cloned.1.call-start
  7.3 0.9 fusion.45
  8.2 1.1 broadcast_multiply_fusion
  9.3 28.8 %all-gather = bf16[1,2048,128]{2,1,0:T(8,128)(2,1)S(1)} all-gather(bf16[1,256,128]{2,1,0:T(8,128)(2,1)S(1)} %get-tuple-element.14), channel_id=2, replica_groups=mesh['prow'=4,'pcol'=8] {'pcol'}, dimensions={1}, use_global_device_ids=true | all-gather | bytes 589824 | tf_op jit(solution)/shard_map/all_gather | solution.py:31
  38.0 31.6 %all-gather.2 = bf16[1,2048,128]{2,1,0:T(8,128)(2,1)S(1)} all-gather(bf16[1,256,128]{2,1,0:T(8,128)(2,1)S(1)} %get-tuple-element.15), channel_id=4, replica_groups=mesh['prow'=4,'pcol'=8] {'pcol'}, dimensions={1}, use_global_device_ids=true | all-gather | bytes 589824 | tf_op jit(solution)/shard_map/all_gather | solution.py:31
  69.6 0.8 select_bitcast_fusion.2
  70.4 0.8 select_bitcast_fusion
  71.2 31.1 %all-gather.1 = bf16[1,2048,128]{2,1,0:T(8,128)(2,1)S(1)} all-gather(bf16[1,256,128]{2,1,0:T(8,128)(2,1)S(1)} %get-tuple-element.16), channel_id=3, replica_groups=mesh['prow'=4,'pcol'=8] {'pcol'}, dimensions={1}, use_global_device_ids=true | all-gather | bytes 589824 | tf_op jit(solution)/shard_map/all_gather | solution.py:31
  102.3 0.8 select_bitcast_fusion.1
  103.0 0.0 all-reduce.7.cloned.1.call-update
  103.1 0.0 reduce-scatter.6.cloned.1.call-start
  103.1 39.1 %all-reduce.7.cloned.1.call-done = (bf16[1024,128]{1,0:T(8,128)(2,1)}, bf16[1024,128]{1,0:T(8,128)(2,1)}, bf16[1024,128]{1,0:T(8,128)(2,1)}) async-done(((bf16[1024,128]{1,0:T(8,128)(2,1)}, bf16[1024,128]{1,0:T(8,128)(2,1)}, bf16[1024,128]{1,0:T(8,128)(2,1)}), (bf16[1024,128]{1,0:T(8,128)(2,1)}, bf16[1024,128]{1,0:T(8,128)(2,1)}, bf16[1024,128]{1,0:T(8,128)(2,1)})) %all-reduce.7.cloned.1.call-update) | async-done | bytes 786448 | tf_op jit(solution)/shard_map/psum | solution.py:9
  142.2 0.0 copy-start.3
  142.2 4.8 convolution_bitcast_fusion.1
  147.0 0.0 reduce-scatter.6.cloned.1.call-update
  147.0 0.0 reduce-scatter.4.cloned.1.call-start
  147.1 0.0 copy-done.3
  147.1 4.7 convolution_bitcast_fusion.2
  151.8 0.0 reduce-scatter.4.cloned.1.call-update
  151.8 0.0 reduce-scatter.8.cloned.1.call-start
  151.9 0.0 copy-done.2
  151.9 0.0 copy-start.1
  151.9 4.8 convolution_bitcast_fusion
  156.7 0.0 reduce-scatter.8.cloned.1.call-update
  156.7 0.0 all-reduce.5.cloned.1.call-start
  156.7 54.9 %reduce-scatter.6.cloned.1.call-done = f32[256,128]{0,1:T(8,128)} async-done(((f32[2048,128]{0,1:T(8,128)}), f32[256,128]{0,1:T(8,128)}) %reduce-scatter.6.cloned.1.call-update) | async-done | bytes 131088 | tf_op jit(solution)/shard_map/reduce_scatter | solution.py:39
  211.7 67.1 %reduce-scatter.4.cloned.1.call-done = f32[256,128]{0,1:T(8,128)} async-done(((f32[2048,128]{0,1:T(8,128)}), f32[256,128]{0,1:T(8,128)}) %reduce-scatter.4.cloned.1.call-update) | async-done | bytes 131088 | tf_op jit(solution)/shard_map/reduce_scatter | solution.py:39
  278.8 0.0 copy-done
  278.8 1.2 fusion.2
  280.0 0.9 fusion.18
  280.9 0.8 fusion.12
  281.7 64.0 %reduce-scatter.8.cloned.1.call-done = f32[256,128]{0,1:T(8,128)} async-done(((f32[2048,128]{0,1:T(8,128)}), f32[256,128]{0,1:T(8,128)}) %reduce-scatter.8.cloned.1.call-update) | async-done | bytes 131088 | tf_op jit(solution)/shard_map/reduce_scatter | solution.py:39
  345.7 1.2 fusion.3
  346.9 0.9 fusion.14
  347.8 1.7 fusion.10
  349.5 1.8 fusion.9
  351.3 0.0 all-reduce.5.cloned.1.call-update
  351.3 0.9 fusion.11
  352.3 0.9 copy.12
  353.2 129.2 %all-reduce.5.cloned.1.call-done = (f32[128,128]{1,0:T(8,128)}, f32[128,128]{1,0:T(8,128)}, f32[128,128]{1,0:T(8,128)}, f32[128,128]{1,0:T(8,128)}, f32[128,128]{1,0:T(8,128)}) async-done(((f32[128,128]{1,0:T(8,128)}, f32[128,128]{1,0:T(8,128)}, f32[128,128]{1,0:T(8,128)}, f32[128,128]{1,0:T(8,128)}, f32[128,128]{1,0:T(8,128)}), (f32[128,128]{1,0:T(8,128)}, f32[128,128]{1,0:T(8,128)}, f32[128,128]{1,0:T(8,128)}, ...) | async-done | bytes 327696 | tf_op jit(solution)/shard_map/psum | solution.py:62
  482.4 0.0 copy-done.1
  482.4 0.8 fusion.30
  483.2 1.0 fusion.8
  484.3 1.1 fusion.7
  485.4 1.0 fusion.6
  486.4 1.1 fusion.5
  487.5 0.7 pad_maximum_fusion.2
  488.2 0.7 pad_maximum_fusion.1
  (6 shorter events, 0.1 us)
Async XLA Ops:
  7.2 135.0 %all-reduce.7.cloned.1.call-start = ((), (), s32[]{:S(2)}) async-start(), calls=%async_computation.7 | async-start | bytes 1572864 | tf_op jit(solution)/shard_map/psum | solution.py:9
  103.1 108.6 %reduce-scatter.6.cloned.1.call-start = ((), (), s32[]{:S(2)}) async-start(), calls=%async_computation.4 | async-start | bytes 1179648 | tf_op jit(solution)/shard_map/reduce_scatter | solution.py:39
  142.2 4.9 copy-start.3
  147.0 4.9 copy-start.2
  147.0 131.7 %reduce-scatter.4.cloned.1.call-start = ((), (), s32[]{:S(2)}) async-start(), calls=%async_computation.3 | async-start | bytes 1179648 | tf_op jit(solution)/shard_map/reduce_scatter | solution.py:39
  151.8 127.0 %copy-start = (bf16[2,128,128]{2,1,0:T(8,128)(2,1)S(1)}, bf16[2,128,128]{2,1,0:T(8,128)(2,1)}, u32[]{:S(2)}) copy-start(bf16[2,128,128]{2,1,0:T(8,128)(2,1)} %param.9) | copy-start | bytes 196612
  151.8 193.9 %reduce-scatter.8.cloned.1.call-start = ((), (), s32[]{:S(2)}) async-start(), calls=%async_computation.5 | async-start | bytes 1179648 | tf_op jit(solution)/shard_map/reduce_scatter | solution.py:39
  151.9 330.5 %copy-start.1 = (f32[3,128,128]{2,1,0:T(8,128)S(1)}, f32[3,128,128]{2,1,0:T(8,128)}, u32[]{:S(2)}) copy-start(f32[3,128,128]{2,1,0:T(8,128)} %param.8) | copy-start | bytes 589828
  156.7 325.7 %all-reduce.5.cloned.1.call-start = ((), (), s32[]{:S(2)}) async-start(), calls=%async_computation.6 | async-start | bytes 655360 | tf_op jit(solution)/shard_map/psum | solution.py:62
Sparse Core Ops, SparseCore 0:
  103.2 38.9 all-reduce.6
  147.2 64.4 reduce-scatter.5
  215.1 63.6 reduce-scatter.3
  282.0 63.6 reduce-scatter.7
  352.4 129.9 all-reduce.4
where the time goes:
time: 496 us; the launch traced here: 495 us
  waiting for transfers between devices  354 us (71%)
  blocking collectives  91.5 us (18%)
  matrix products  27.9 us (6%)
  between operations  13.9 us (3%)
  other arithmetic  6.52 us (1%)
    reduce_scatter x3, waiting for transfers between devices, shards(): lax.psum_scatter(single_term(jnp.int32(0), seg_rows * lax.axis_size('pcol...  186 us
    psum x1, waiting for transfers between devices, shards(): own_sum, cross_sum = lax.psum((own_term, cross_term), ('prow', 'pcol'))  129 us
    all_gather x3, blocking collectives, shards(): gathered = lax.all_gather(factor[section], 'pcol', axis=0, tiled=True)  91.5 us
    psum x1, waiting for transfers between devices, broadcast(): return lax.psum(kept, axis)  39.1 us
    dot_general x3, matrix products, single_term(): return jnp.dot(ainv, panel_cols, preferred_element_type=jnp.float32)  14.3 us
  transfers between devices with their start and end apart: 5, of which 5 were waited for; matrix products, arithmetic and copies ran while one was open for 3% of the time, Pallas kernels for 0%

commit v1 on v0

--- a/solution.py
+++ b/solution.py
@@ -2,6 +2,28 @@
 import jax.numpy as jnp
 from jax import lax
 from jax.sharding import PartitionSpec as P
+
+
+def in_order(blocks, dim):
+    blocks = jnp.moveaxis(blocks, 0, dim)
+    shape = blocks.shape
+    return blocks.reshape(*shape[:dim], shape[dim] * shape[dim + 1], *shape[dim + 2 :])
+
+
+def ring_gather(value, axis, dim):
+    devices = lax.axis_size(axis)
+    pairs = [(i, (i + 1) % devices) for i in range(devices)]
+    back = [(b, a) for a, b in pairs]
+    lower, upper = ([], [])
+    for step in range(devices - 1):
+        if step % 2 == 0:
+            lower.append(lax.ppermute(lower[-1] if lower else value, axis, pairs))
+        else:
+            upper.append(lax.ppermute(upper[-1] if upper else value, axis, back))
+    blocks = jnp.stack([*lower[::-1], value, *upper])
+    shift = lax.axis_index(axis) - len(lower)
+    blocks = blocks[(jnp.arange(devices) - shift) % devices]
+    return in_order(blocks, dim)
 
 
 def broadcast(value, axis, source):
@@ -28,7 +50,7 @@
     owner = column * col_span // height
     products = []
     for section in range(sections):
-        gathered = lax.all_gather(factor[section], "pcol", axis=0, tiled=True)
+        gathered = ring_gather(factor[section], "pcol", 0)
         wanted = lax.dynamic_slice_in_dim(gathered, offset, col_span, 0)
         received = broadcast(wanted, "prow", owner)
 

time: 496 us -> 440 us (0.89)
  blocking collectives: 91.5 us -> 0 us
  starting transfers between devices: 0.21 us -> 29.5 us
  waiting for transfers between devices: 354 us -> 359 us
    all_gather x3 -> x0, blocking collectives: 91.5 us -> none  [shards(): gathered = lax.all_gather(factor[section], 'pcol', axis=0, tiled=True)]
    ppermute x0 -> x21, starting transfers between devices: none -> 29.3 us  [the longest x9 15.8 us: ring_gather(): upper.append(lax.ppermute(upper[-1] if upper else value, axis, back))]
    ppermute x0 -> x21, waiting for transfers between devices: none -> 8.57 us  [the longest x12 5.69 us: ring_gather(): lower.append(lax.ppermute(lower[-1] if lower else value, axis, pairs))]
  transfers between devices with their start and end apart: 5 -> 26, of which waited for: 5 -> 9; matrix products, arithmetic and copies ran while one was open for 3% -> 4% of each run, Pallas kernels for 0% -> 0%
where the time goes in v1:
time: 440 us
  waiting for transfers between devices  359 us (82%)
  starting transfers between devices  29.5 us (7%)
  matrix products  27.9 us (6%)
  between operations  14.1 us (3%)
  other arithmetic  5.92 us (1%)
    reduce_scatter x3, waiting for transfers between devices, shards(): lax.psum_scatter(single_term(jnp.int32(0), seg_rows * lax.axis_size('pcol...  186 us
    psum x1, waiting for transfers between devices, shards(): own_sum, cross_sum = lax.psum((own_term, cross_term), ('prow', 'pcol'))  129 us
    psum x1, waiting for transfers between devices, broadcast(): return lax.psum(kept, axis)  35.1 us
    ppermute x9, starting transfers between devices, ring_gather(): upper.append(lax.ppermute(upper[-1] if upper else value, axis, back))  15.8 us
    dot_general x3, matrix products, single_term(): return jnp.dot(ainv, panel_cols, preferred_element_type=jnp.float32)  14.3 us
    ppermute x12, starting transfers between devices, ring_gather(): lower.append(lax.ppermute(lower[-1] if lower else value, axis, pairs))  13.5 us
  transfers between devices with their start and end apart: 26, of which 9 were waited for; matrix products, arithmetic and copies ran while one was open for 4% of the time, Pallas kernels for 0%

profile of v1, /device:TPU:8, one launch (start us, length us, event | category | flops | bytes accessed | tf_op | source)
XLA Modules:
  0.0 439.6 jit_solution(11782098868727066701)
XLA Ops:
  7.2 0.9 fusion.36
  8.1 1.1 broadcast_multiply_fusion
  9.3 1.5 collective-permute-start.7
  10.8 1.5 collective-permute-start.14
  12.4 1.5 collective-permute-start
  13.8 1.4 collective-permute-start.11
  15.8 1.5 collective-permute-start.8
  17.3 1.7 collective-permute-start.4
  19.6 2.1 collective-permute-start.1
  21.7 0.7 collective-permute-done.18
  22.6 1.9 collective-permute-start.9
  24.5 2.2 collective-permute-done.4
  26.7 2.4 collective-permute-start.5
  29.1 2.5 collective-permute-start.2
  31.8 2.8 collective-permute-start.13
  34.6 4.2 collective-permute-start.20
  38.8 2.6 collective-permute-start.6
  41.5 5.0 %collective-permute-done.17 = bf16[256,128]{1,0:T(8,128)(2,1)S(1)} collective-permute-done((bf16[256,128]{1,0:T(8,128)(2,1)S(1)}, bf16[256,128]{1,0:T(8,128)(2,1)S(1)}, u32[]{:S(2)}, u32[]{:S(2)}) %collective-permute-start.17) | collective-permute-done | bytes 65568 | tf_op jit(solution)/shard_map/ppermute | solution.py:20
  46.6 0.6 collective-permute-done.3
  47.5 0.6 gather_fusion.1
  48.2 0.6 gather_fusion.2
  48.9 0.6 gather_fusion
  49.5 0.8 dynamic-slice_select_fusion.2
  50.3 0.9 dynamic-slice_select_fusion
  51.2 35.1 %all-reduce.7.cloned.1.call-done = (bf16[1024,128]{1,0:T(8,128)(2,1)}, bf16[1024,128]{1,0:T(8,128)(2,1)}, bf16[1024,128]{1,0:T(8,128)(2,1)}) async-done(((bf16[1024,128]{1,0:T(8,128)(2,1)}, bf16[1024,128]{1,0:T(8,128)(2,1)}, bf16[1024,128]{1,0:T(8,128)(2,1)}), (bf16[1024,128]{1,0:T(8,128)(2,1)}, bf16[1024,128]{1,0:T(8,128)(2,1)}, bf16[1024,128]{1,0:T(8,128)(2,1)})) %all-reduce.7.cloned.1.call-update) | async-done | bytes 786448 | tf_op jit(solution)/shard_map/psum | solution.py:31
  86.4 4.8 %convolution_bitcast_fusion.2 = f32[2048,128]{0,1:T(8,128)} fusion(bf16[1024,128]{1,0:T(8,128)(2,1)} %get-tuple-element.13, bf16[2048,1024]{1,0:T(8,128)(2,1)} %param.5), kind=kOutput, calls=%fused_computation.5 | convolution fusion | flops 536870912 | bytes 5505024 | tf_op jit(solution)/shard_map/dot_general | solution.py:58
  91.3 4.7 %convolution_bitcast_fusion.1 = f32[2048,128]{0,1:T(8,128)} fusion(bf16[1024,128]{1,0:T(8,128)(2,1)S(1)} %copy-done.3, bf16[2048,1024]{1,0:T(8,128)(2,1)} %param.5), kind=kOutput, calls=%fused_computation.4 | convolution fusion | flops 536870912 | bytes 5505024 | tf_op jit(solution)/shard_map/dot_general | solution.py:58
  96.1 4.7 %convolution_bitcast_fusion = f32[2048,128]{0,1:T(8,128)} fusion(bf16[1024,128]{1,0:T(8,128)(2,1)S(1)} %copy-done.2, bf16[2048,1024]{1,0:T(8,128)(2,1)} %param.5), kind=kOutput, calls=%fused_computation.3 | convolution fusion | flops 536870912 | bytes 5505024 | tf_op jit(solution)/shard_map/dot_general | solution.py:58
  100.9 55.0 %reduce-scatter.4.cloned.1.call-done = f32[256,128]{0,1:T(8,128)} async-done(((f32[2048,128]{0,1:T(8,128)}), f32[256,128]{0,1:T(8,128)}) %reduce-scatter.4.cloned.1.call-update) | async-done | bytes 131088 | tf_op jit(solution)/shard_map/reduce_scatter | solution.py:61
  155.9 67.1 %reduce-scatter.6.cloned.1.call-done = f32[256,128]{0,1:T(8,128)} async-done(((f32[2048,128]{0,1:T(8,128)}), f32[256,128]{0,1:T(8,128)}) %reduce-scatter.6.cloned.1.call-update) | async-done | bytes 131088 | tf_op jit(solution)/shard_map/reduce_scatter | solution.py:61
  223.1 1.2 fusion.2
  224.3 0.9 fusion.32
  225.2 0.8 fusion.34
  226.0 64.0 %reduce-scatter.8.cloned.1.call-done = f32[256,128]{0,1:T(8,128)} async-done(((f32[2048,128]{0,1:T(8,128)}), f32[256,128]{0,1:T(8,128)}) %reduce-scatter.8.cloned.1.call-update) | async-done | bytes 131088 | tf_op jit(solution)/shard_map/reduce_scatter | solution.py:61
  290.0 1.2 fusion.3
  291.2 0.9 fusion.33
  292.1 1.7 fusion.10
  293.8 1.8 fusion.9
  295.6 0.9 fusion.11
  296.6 0.9 copy.12
  297.5 129.1 %all-reduce.5.cloned.1.call-done = (f32[128,128]{1,0:T(8,128)}, f32[128,128]{1,0:T(8,128)}, f32[128,128]{1,0:T(8,128)}, f32[128,128]{1,0:T(8,128)}, f32[128,128]{1,0:T(8,128)}) async-done(((f32[128,128]{1,0:T(8,128)}, f32[128,128]{1,0:T(8,128)}, f32[128,128]{1,0:T(8,128)}, f32[128,128]{1,0:T(8,128)}, f32[128,128]{1,0:T(8,128)}), (f32[128,128]{1,0:T(8,128)}, f32[128,128]{1,0:T(8,128)}, f32[128,128]{1,0:T(8,128)}, ...) | async-done | bytes 327696 | tf_op jit(solution)/shard_map/psum | solution.py:84
  426.6 0.8 fusion.22
  427.4 1.0 fusion.8
  428.5 1.1 fusion.7
  429.6 1.0 fusion.6
  430.6 1.1 fusion.5
  431.7 0.7 pad_maximum_fusion.2
  432.4 0.7 pad_maximum_fusion.1
  (71 shorter events, 2.2 us)
Async XLA Ops:
  7.2 79.2 %all-reduce.7.cloned.1.call-start = ((), (), s32[]{:S(2)}) async-start(), calls=%async_computation.7 | async-start | bytes 1572864 | tf_op jit(solution)/shard_map/psum | solution.py:31
  9.3 6.5 %collective-permute-start.7 = (bf16[256,128]{1,0:T(8,128)(2,1)S(1)}, bf16[256,128]{1,0:T(8,128)(2,1)S(1)}, u32[]{:S(2)}, u32[]{:S(2)}) collective-permute-start(bf16[256,128]{1,0:T(8,128)(2,1)S(1)} %get-tuple-element.19), channel_id=1, source_target_pairs={{0,1},{1,2},{2,3},{3,4},{4,5},{5,6},{6,7},{7,0},{8,9},{9,10},{10,1... | collective-permute-start | bytes 196616 | tf_op jit(solution)/shard_map/ppermute | solution.py:20
  10.8 6.5 %collective-permute-start.14 = (bf16[256,128]{1,0:T(8,128)(2,1)S(1)}, bf16[256,128]{1,0:T(8,128)(2,1)S(1)}, u32[]{:S(2)}, u32[]{:S(2)}) collective-permute-start(bf16[256,128]{1,0:T(8,128)(2,1)S(1)} %get-tuple-element.18), channel_id=1, source_target_pairs={{0,1},{1,2},{2,3},{3,4},{4,5},{5,6},{6,7},{7,0},{8,9},{9,10},{10,1... | collective-permute-start | bytes 196616 | tf_op jit(solution)/shard_map/ppermute | solution.py:20
  12.4 6.7 %collective-permute-start = (bf16[256,128]{1,0:T(8,128)(2,1)S(1)}, bf16[256,128]{1,0:T(8,128)(2,1)S(1)}, u32[]{:S(2)}, u32[]{:S(2)}) collective-permute-start(bf16[256,128]{1,0:T(8,128)(2,1)S(1)} %get-tuple-element.17), channel_id=1, source_target_pairs={{0,1},{1,2},{2,3},{3,4},{4,5},{5,6},{6,7},{7,0},{8,9},{9,10},{10,1... | collective-permute-start | bytes 196616 | tf_op jit(solution)/shard_map/ppermute | solution.py:20
  13.8 5.8 %collective-permute-start.11 = (bf16[256,128]{1,0:T(8,128)(2,1)S(1)}, bf16[256,128]{1,0:T(8,128)(2,1)S(1)}, u32[]{:S(2)}, u32[]{:S(2)}) collective-permute-start(bf16[256,128]{1,0:T(8,128)(2,1)S(1)} %get-tuple-element.19), channel_id=1, source_target_pairs={{1,0},{2,1},{3,2},{4,3},{5,4},{6,5},{7,6},{0,7},{9,8},{10,9},{11,1... | collective-permute-start | bytes 196616 | tf_op jit(solution)/shard_map/ppermute | solution.py:22
  15.3 7.2 %collective-permute-start.18 = (bf16[256,128]{1,0:T(8,128)(2,1)S(1)}, bf16[256,128]{1,0:T(8,128)(2,1)S(1)}, u32[]{:S(2)}, u32[]{:S(2)}) collective-permute-start(bf16[256,128]{1,0:T(8,128)(2,1)S(1)} %get-tuple-element.18), channel_id=1, source_target_pairs={{1,0},{2,1},{3,2},{4,3},{5,4},{6,5},{7,6},{0,7},{9,8},{10,9},{11,1... | collective-permute-start | bytes 196616 | tf_op jit(solution)/shard_map/ppermute | solution.py:22
  15.8 6.8 %collective-permute-start.8 = (bf16[256,128]{1,0:T(8,128)(2,1)S(1)}, bf16[256,128]{1,0:T(8,128)(2,1)S(1)}, u32[]{:S(2)}, u32[]{:S(2)}) collective-permute-start(bf16[256,128]{1,0:T(8,128)(2,1)S(1)} %collective-permute-done.7), channel_id=1, source_target_pairs={{0,1},{1,2},{2,3},{3,4},{4,5},{5,6},{6,7},{7,0},{8,9},{9,10},{10,1... | collective-permute-start | bytes 196616 | tf_op jit(solution)/shard_map/ppermute | solution.py:20
  17.3 9.3 %collective-permute-start.4 = (bf16[256,128]{1,0:T(8,128)(2,1)S(1)}, bf16[256,128]{1,0:T(8,128)(2,1)S(1)}, u32[]{:S(2)}, u32[]{:S(2)}) collective-permute-start(bf16[256,128]{1,0:T(8,128)(2,1)S(1)} %get-tuple-element.17), channel_id=1, source_target_pairs={{1,0},{2,1},{3,2},{4,3},{5,4},{6,5},{7,6},{0,7},{9,8},{10,9},{11,1... | collective-permute-start | bytes 196616 | tf_op jit(solution)/shard_map/ppermute | solution.py:22
  19.1 7.6 %collective-permute-start.15 = (bf16[256,128]{1,0:T(8,128)(2,1)S(1)}, bf16[256,128]{1,0:T(8,128)(2,1)S(1)}, u32[]{:S(2)}, u32[]{:S(2)}) collective-permute-start(bf16[256,128]{1,0:T(8,128)(2,1)S(1)} %collective-permute-done.14), channel_id=1, source_target_pairs={{0,1},{1,2},{2,3},{3,4},{4,5},{5,6},{6,7},{7,0},{8,9},{9,10},{10,1... | collective-permute-start | bytes 196616 | tf_op jit(solution)/shard_map/ppermute | solution.py:20
  19.6 9.4 %collective-permute-start.1 = (bf16[256,128]{1,0:T(8,128)(2,1)S(1)}, bf16[256,128]{1,0:T(8,128)(2,1)S(1)}, u32[]{:S(2)}, u32[]{:S(2)}) collective-permute-start(bf16[256,128]{1,0:T(8,128)(2,1)S(1)} %collective-permute-done), channel_id=1, source_target_pairs={{0,1},{1,2},{2,3},{3,4},{4,5},{5,6},{6,7},{7,0},{8,9},{9,10},{10,1... | collective-permute-start | bytes 196616 | tf_op jit(solution)/shard_map/ppermute | solution.py:20
  22.4 6.7 %collective-permute-start.12 = (bf16[256,128]{1,0:T(8,128)(2,1)S(1)}, bf16[256,128]{1,0:T(8,128)(2,1)S(1)}, u32[]{:S(2)}, u32[]{:S(2)}) collective-permute-start(bf16[256,128]{1,0:T(8,128)(2,1)S(1)} %collective-permute-done.11), channel_id=1, source_target_pairs={{1,0},{2,1},{3,2},{4,3},{5,4},{6,5},{7,6},{0,7},{9,8},{10,9},{11,1... | collective-permute-start | bytes 196616 | tf_op jit(solution)/shard_map/ppermute | solution.py:22
  22.6 9.0 %collective-permute-start.9 = (bf16[256,128]{1,0:T(8,128)(2,1)S(1)}, bf16[256,128]{1,0:T(8,128)(2,1)S(1)}, u32[]{:S(2)}, u32[]{:S(2)}) collective-permute-start(bf16[256,128]{1,0:T(8,128)(2,1)S(1)} %collective-permute-done.8), channel_id=1, source_target_pairs={{0,1},{1,2},{2,3},{3,4},{4,5},{5,6},{6,7},{7,0},{8,9},{9,10},{10,1... | collective-permute-start | bytes 196616 | tf_op jit(solution)/shard_map/ppermute | solution.py:20
  26.6 5.2 %collective-permute-start.19 = (bf16[256,128]{1,0:T(8,128)(2,1)S(1)}, bf16[256,128]{1,0:T(8,128)(2,1)S(1)}, u32[]{:S(2)}, u32[]{:S(2)}) collective-permute-start(bf16[256,128]{1,0:T(8,128)(2,1)S(1)} %collective-permute-done.18), channel_id=1, source_target_pairs={{1,0},{2,1},{3,2},{4,3},{5,4},{6,5},{7,6},{0,7},{9,8},{10,9},{11,1... | collective-permute-start | bytes 196616 | tf_op jit(solution)/shard_map/ppermute | solution.py:22
  26.7 8.0 %collective-permute-start.5 = (bf16[256,128]{1,0:T(8,128)(2,1)S(1)}, bf16[256,128]{1,0:T(8,128)(2,1)S(1)}, u32[]{:S(2)}, u32[]{:S(2)}) collective-permute-start(bf16[256,128]{1,0:T(8,128)(2,1)S(1)} %collective-permute-done.4), channel_id=1, source_target_pairs={{1,0},{2,1},{3,2},{4,3},{5,4},{6,5},{7,6},{0,7},{9,8},{10,9},{11,1... | collective-permute-start | bytes 196616 | tf_op jit(solution)/shard_map/ppermute | solution.py:22
  29.1 9.7 %collective-permute-start.16 = (bf16[256,128]{1,0:T(8,128)(2,1)S(1)}, bf16[256,128]{1,0:T(8,128)(2,1)S(1)}, u32[]{:S(2)}, u32[]{:S(2)}) collective-permute-start(bf16[256,128]{1,0:T(8,128)(2,1)S(1)} %collective-permute-done.15), channel_id=1, source_target_pairs={{0,1},{1,2},{2,3},{3,4},{4,5},{5,6},{6,7},{7,0},{8,9},{9,10},{10,1... | collective-permute-start | bytes 196616 | tf_op jit(solution)/shard_map/ppermute | solution.py:20
  29.1 12.3 %collective-permute-start.2 = (bf16[256,128]{1,0:T(8,128)(2,1)S(1)}, bf16[256,128]{1,0:T(8,128)(2,1)S(1)}, u32[]{:S(2)}, u32[]{:S(2)}) collective-permute-start(bf16[256,128]{1,0:T(8,128)(2,1)S(1)} %collective-permute-done.1), channel_id=1, source_target_pairs={{0,1},{1,2},{2,3},{3,4},{4,5},{5,6},{6,7},{7,0},{8,9},{9,10},{10,1... | collective-permute-start | bytes 196616 | tf_op jit(solution)/shard_map/ppermute | solution.py:20
  31.6 9.8 %collective-permute-start.10 = (bf16[256,128]{1,0:T(8,128)(2,1)S(1)}, bf16[256,128]{1,0:T(8,128)(2,1)S(1)}, u32[]{:S(2)}, u32[]{:S(2)}) collective-permute-start(bf16[256,128]{1,0:T(8,128)(2,1)S(1)} %collective-permute-done.9), channel_id=1, source_target_pairs={{0,1},{1,2},{2,3},{3,4},{4,5},{5,6},{6,7},{7,0},{8,9},{9,10},{10,1... | collective-permute-start | bytes 196616 | tf_op jit(solution)/shard_map/ppermute | solution.py:20
  31.8 15.7 %collective-permute-start.13 = (bf16[256,128]{1,0:T(8,128)(2,1)S(1)}, bf16[256,128]{1,0:T(8,128)(2,1)S(1)}, u32[]{:S(2)}, u32[]{:S(2)}) collective-permute-start(bf16[256,128]{1,0:T(8,128)(2,1)S(1)} %collective-permute-done.12), channel_id=1, source_target_pairs={{1,0},{2,1},{3,2},{4,3},{5,4},{6,5},{7,6},{0,7},{9,8},{10,9},{11,1... | collective-permute-start | bytes 196616 | tf_op jit(solution)/shard_map/ppermute | solution.py:22
  34.6 12.9 %collective-permute-start.20 = (bf16[256,128]{1,0:T(8,128)(2,1)S(1)}, bf16[256,128]{1,0:T(8,128)(2,1)S(1)}, u32[]{:S(2)}, u32[]{:S(2)}) collective-permute-start(bf16[256,128]{1,0:T(8,128)(2,1)S(1)} %collective-permute-done.19), channel_id=1, source_target_pairs={{1,0},{2,1},{3,2},{4,3},{5,4},{6,5},{7,6},{0,7},{9,8},{10,9},{11,1... | collective-permute-start | bytes 196616 | tf_op jit(solution)/shard_map/ppermute | solution.py:22
  38.8 10.1 %collective-permute-start.6 = (bf16[256,128]{1,0:T(8,128)(2,1)S(1)}, bf16[256,128]{1,0:T(8,128)(2,1)S(1)}, u32[]{:S(2)}, u32[]{:S(2)}) collective-permute-start(bf16[256,128]{1,0:T(8,128)(2,1)S(1)} %collective-permute-done.5), channel_id=1, source_target_pairs={{1,0},{2,1},{3,2},{4,3},{5,4},{6,5},{7,6},{0,7},{9,8},{10,9},{11,1... | collective-permute-start | bytes 196616 | tf_op jit(solution)/shard_map/ppermute | solution.py:22
  41.4 5.2 %collective-permute-start.17 = (bf16[256,128]{1,0:T(8,128)(2,1)S(1)}, bf16[256,128]{1,0:T(8,128)(2,1)S(1)}, u32[]{:S(2)}, u32[]{:S(2)}) collective-permute-start(bf16[256,128]{1,0:T(8,128)(2,1)S(1)} %collective-permute-done.16), channel_id=1, source_target_pairs={{0,1},{1,2},{2,3},{3,4},{4,5},{5,6},{6,7},{7,0},{8,9},{9,10},{10,1... | collective-permute-start | bytes 196616 | tf_op jit(solution)/shard_map/ppermute | solution.py:20
  41.4 5.9 %collective-permute-start.3 = (bf16[256,128]{1,0:T(8,128)(2,1)S(1)}, bf16[256,128]{1,0:T(8,128)(2,1)S(1)}, u32[]{:S(2)}, u32[]{:S(2)}) collective-permute-start(bf16[256,128]{1,0:T(8,128)(2,1)S(1)} %collective-permute-done.2), channel_id=1, source_target_pairs={{0,1},{1,2},{2,3},{3,4},{4,5},{5,6},{6,7},{7,0},{8,9},{9,10},{10,1... | collective-permute-start | bytes 196616 | tf_op jit(solution)/shard_map/ppermute | solution.py:20
  51.2 104.8 %reduce-scatter.4.cloned.1.call-start = ((), (), s32[]{:S(2)}) async-start(), calls=%async_computation.3 | async-start | bytes 1179648 | tf_op jit(solution)/shard_map/reduce_scatter | solution.py:61
  86.4 4.9 %copy-start.3 = (bf16[1024,128]{1,0:T(8,128)(2,1)S(1)}, bf16[1024,128]{1,0:T(8,128)(2,1)}, u32[]{:S(2)}) copy-start(bf16[1024,128]{1,0:T(8,128)(2,1)} %get-tuple-element.12) | copy-start | bytes 786436
  91.2 4.9 %copy-start.2 = (bf16[1024,128]{1,0:T(8,128)(2,1)S(1)}, bf16[1024,128]{1,0:T(8,128)(2,1)}, u32[]{:S(2)}) copy-start(bf16[1024,128]{1,0:T(8,128)(2,1)} %get-tuple-element.11) | copy-start | bytes 786436
  91.2 131.8 %reduce-scatter.6.cloned.1.call-start = ((), (), s32[]{:S(2)}) async-start(), calls=%async_computation.4 | async-start | bytes 1179648 | tf_op jit(solution)/shard_map/reduce_scatter | solution.py:61
  96.0 127.0 %copy-start = (bf16[2,128,128]{2,1,0:T(8,128)(2,1)S(1)}, bf16[2,128,128]{2,1,0:T(8,128)(2,1)}, u32[]{:S(2)}) copy-start(bf16[2,128,128]{2,1,0:T(8,128)(2,1)} %param.9) | copy-start | bytes 196612
  96.0 194.0 %reduce-scatter.8.cloned.1.call-start = ((), (), s32[]{:S(2)}) async-start(), calls=%async_computation.5 | async-start | bytes 1179648 | tf_op jit(solution)/shard_map/reduce_scatter | solution.py:61
  96.1 330.5 %copy-start.1 = (f32[3,128,128]{2,1,0:T(8,128)S(1)}, f32[3,128,128]{2,1,0:T(8,128)}, u32[]{:S(2)}) copy-start(f32[3,128,128]{2,1,0:T(8,128)} %param.8) | copy-start | bytes 589828
  100.9 325.7 %all-reduce.5.cloned.1.call-start = ((), (), s32[]{:S(2)}) async-start(), calls=%async_computation.6 | async-start | bytes 655360 | tf_op jit(solution)/shard_map/psum | solution.py:84
Sparse Core Ops, SparseCore 0:
  51.3 35.0 all-reduce.6
  91.4 64.5 reduce-scatter.3
  159.4 63.6 reduce-scatter.5
  226.3 63.6 reduce-scatter.7
  296.6 129.9 all-reduce.4
